TPU v7x, 32 devices: a whole 2x2x4 slice. The times are simulated.
32 devices in a mesh: row: 8 (over z, x), col: 2 (over core), rank: 2 (over y).
Axes of the slice: x: 2, y: 2, z: 4, core: 2. Of those that a mesh axis runs over, the one named last changes fastest.
Arguments:
- tensor: bfloat16 [64, 2048, 2048], P(None, 'row', 'col'), may hold values from -6 to 6
- aux_factor: bfloat16 [64, 256], P(None, 'rank'), may hold values from -0.75 to 0.75
- row_factor: bfloat16 [2048, 256], P(('row', 'col'), 'rank'), may hold values from -0.125 to 0.125
- col_factor: bfloat16 [2048, 256], P(('col', 'row'), 'rank'), may hold values from -0.125 to 0.125
Outputs:
- row_result: float32 [2048, 256], P(('row', 'col'), 'rank')
- aux_result: float32 [64, 256], P('row', 'rank')
All inputs are finite; a program needn't handle non-finite values.
Results may differ from a plain program's by a relative error of at most 0.0003.
Values may be sent and summed in bfloat16 or wider, within the bound.
A program may use at most 128 MiB of HBM per device.

v0:
```python
import functools

import jax
import jax.numpy as jnp
from jax import lax
from jax.experimental import pallas as pl
from jax.experimental.pallas import tpu as pltpu
from jax.sharding import PartitionSpec as P

MESH = pl.DeviceIdType.MESH
f32 = jnp.float32


def kernel(R, C, tensor, aux, rowf, colf, out,
           tbuf, colbuf, rowbuf, auxbuf, row_panel, aux_panel, row_acc, aux_acc, inner_acc, row_in, aux_in,
           t_sem, c_send, c_recv, r_send, r_recv, l_sem, a_send, a_recv, p_send, p_recv, far_sem):
    r = lax.axis_index("row")
    c = lax.axis_index("col")
    other = 1 - c
    A, I, J = tensor.shape
    N = colf.shape[1]
    jb = colf.shape[0]
    ib = rowf.shape[0]
    ac = A // R
    H = R // 2
    jh = J // 2
    half = r // H

    def chunk_of(s):
        return lax.rem(r + 1 + s, R)

    def load(p, s):
        k = chunk_of(s)
        h = half if p == 0 else 1 - half
        cols = pl.ds(pl.multiple_of(h * jh, jh), jh)
        return pltpu.make_async_copy(
            tensor.at[pl.ds(k * ac, ac), :, cols], tbuf.at[p, k], t_sem.at[p, s])

    own_col = pltpu.make_async_copy(colf, colbuf.at[r], l_sem.at[0])
    own_row = pltpu.make_async_copy(rowf, rowbuf.at[c], l_sem.at[1])
    own_aux = pltpu.make_async_copy(aux, auxbuf, l_sem.at[2])
    own_col.start()
    own_row.start()
    own_aux.start()

    barrier = pltpu.get_barrier_semaphore()
    near = [half * H + lax.rem(lax.rem(r, H) + d, H) for d in range(1, H)]
    far = [(1 - half) * H + lax.rem(lax.rem(r, H) + d, H) for d in range(H)]
    x = lax.rem(r, 2)
    gate = jnp.where(half == 0, H - 2, H) + x
    beyond = jnp.where(half == 0, H, H - 2) + x
    at_gate = r == gate

    def signal(sem, where):
        pl.semaphore_signal(sem, inc=1, device_id=where, device_id_type=MESH)

    signal(barrier, {"col": other})
    for target in near:
        signal(barrier, {"row": target})

    @pl.when(at_gate)
    def _():
        signal(barrier, {"row": beyond})

    own_col.wait()
    own_row.wait()
    own_aux.wait()
    for p in range(2):
        for s in range(R):
            load(p, s).start()
    pl.semaphore_wait(barrier, H + jnp.where(at_gate, 1, 0))

    def col_copy(target):
        return pltpu.make_async_remote_copy(
            src_ref=colbuf.at[r], dst_ref=colbuf.at[r], send_sem=c_send.at[target], recv_sem=c_recv.at[r],
            device_id={"row": target}, device_id_type=MESH)

    def col_arrival(source):
        return pltpu.make_async_remote_copy(
            src_ref=colf, dst_ref=colbuf.at[source], send_sem=c_send.at[source], recv_sem=c_recv.at[source],
            device_id={"row": source}, device_id_type=MESH)

    for target in near:
        col_copy(target).start()
    row_copy = pltpu.make_async_remote_copy(
        src_ref=rowbuf.at[c], dst_ref=rowbuf.at[c], send_sem=r_send, recv_sem=r_recv,
        device_id={"col": other}, device_id_type=MESH)
    row_copy.start()

    @pl.when(at_gate)
    def _():
        signal(far_sem, {"row": beyond})

    pl.semaphore_wait(far_sem, 1)

    @pl.when(at_gate)
    def _():
        for d in range(1, H // 2):
            signal(far_sem, {"row": half * H + lax.rem(lax.rem(r, H) + 2 * d, H)})

    for target in far:
        col_copy(target).start()

    row_acc[...] = jnp.zeros_like(row_acc)
    aux_panel[...] = auxbuf[...].astype(f32).reshape(R, ac, N)
    row_copy.wait()
    row_panel[...] = rowbuf[...].reshape(C * ib, N).astype(f32)
    for source in near:
        col_arrival(source).wait_recv()

    def product(p, s):
        load(p, s).wait()
        k = chunk_of(s)
        h = half if p == 0 else 1 - half
        weights = colbuf[pl.ds(h * H, H)].reshape(H * jb, N)
        return k, jnp.dot(tbuf[p, k].reshape(ac * I, jh), weights, preferred_element_type=f32)

    def block(s):
        k, inner = product(1, s)
        inner = (inner_acc[k] + inner).reshape(ac, I, N)
        row_acc[...] += jnp.sum(inner * aux_panel[k][:, None, :], axis=0)
        aux_acc[k] = jnp.sum(inner * row_panel[...][None], axis=1)
        return k

    def aux_copy(k, e):
        return pltpu.make_async_remote_copy(
            src_ref=aux_acc.at[k], dst_ref=aux_in.at[r, c], send_sem=a_send.at[k, e], recv_sem=a_recv.at[r, c],
            device_id={"row": k, "col": e}, device_id_type=MESH)

    def aux_arrival(source, e):
        return pltpu.make_async_remote_copy(
            src_ref=aux_acc.at[source], dst_ref=aux_in.at[source, e], send_sem=a_send.at[source, e],
            recv_sem=a_recv.at[source, e], device_id={"row": source, "col": e}, device_id_type=MESH)

    def first(s, _):
        k, inner = product(0, s)
        inner_acc[k] = inner
        return 0

    lax.fori_loop(0, R, first, 0)
    for source in far:
        col_arrival(source).wait_recv()

    def second(s, _):
        k = block(s)
        aux_copy(k, c).start()
        aux_copy(k, other).start()
        return 0

    lax.fori_loop(0, R - 1, second, 0)
    block(R - 1)
    part_copy = pltpu.make_async_remote_copy(
        src_ref=row_acc.at[pl.ds(other * ib, ib)], dst_ref=row_in, send_sem=p_send, recv_sem=p_recv,
        device_id={"col": other}, device_id_type=MESH)
    part_copy.start()
    aux_copy(r, other).start()
    aux_in[r, c] = aux_acc[r]
    for d in range(1, R):
        source = lax.rem(r + d, R)
        for e in range(C):
            aux_arrival(source, e).wait_recv()
    aux_arrival(r, other).wait_recv()
    out[ib:, :] = jnp.sum(aux_in[...].reshape(R * C, ac, N), axis=0)
    part_copy.wait_recv()
    out[:ib, :] = row_acc[pl.ds(c * ib, ib)] + row_in[...]

    part_copy.wait_send()
    aux_copy(r, other).wait_send()
    for d in range(1, R):
        k = lax.rem(r + d, R)
        col_copy(k).wait_send()
        for e in range(C):
            aux_copy(k, e).wait_send()


def split(both, row_out, aux_out):
    rows = row_out.shape[0]
    row_out[...] = both[:rows, :]
    aux_out[...] = both[rows:, :]


def fused(R, C, tensor, aux, rowf, colf):
    A, I, J = tensor.shape
    jb, N = colf.shape
    ib = rowf.shape[0]
    ac = A // R
    bf16 = tensor.dtype
    anywhere = pl.BlockSpec(memory_space=pltpu.HBM)
    vmem = pl.BlockSpec(memory_space=pltpu.VMEM)
    dma = pltpu.SemaphoreType.DMA
    both = pl.pallas_call(
        functools.partial(kernel, R, C),
        out_shape=jax.ShapeDtypeStruct((ib + ac, N), f32),
        in_specs=[anywhere] * 4,
        out_specs=vmem,
        scratch_shapes=[
            pltpu.VMEM((2, R, ac, I, J // 2), bf16),
            pltpu.VMEM((R, jb, N), bf16),
            pltpu.VMEM((C, ib, N), bf16),
            pltpu.VMEM((A, N), bf16),
            pltpu.VMEM((C * ib, N), f32),
            pltpu.VMEM((R, ac, N), f32),
            pltpu.VMEM((C * ib, N), f32),
            pltpu.VMEM((R, ac, N), f32),
            pltpu.VMEM((R, ac * I, N), f32),
            pltpu.VMEM((ib, N), f32),
            pltpu.VMEM((R, C, ac, N), f32),
            dma((2, R)), dma((R,)), dma((R,)), dma, dma, dma((3,)),
            dma((R, C)), dma((R, C)), dma, dma, pltpu.SemaphoreType.REGULAR,
        ],
        compiler_params=pltpu.CompilerParams(
            collective_id=0, has_side_effects=True, vmem_limit_bytes=56 * 2**20),
    )(tensor, aux, rowf, colf)
    return pl.pallas_call(
        split,
        out_shape=(jax.ShapeDtypeStruct((ib, N), f32), jax.ShapeDtypeStruct((ac, N), f32)),
        in_specs=[vmem],
        out_specs=(vmem, vmem),
    )(both)


def plain(tensor, aux_factor, row_factor, col_factor):
    row_panel = lax.all_gather(row_factor, "col", axis=0, tiled=True).astype(f32)
    columns = lax.all_gather(col_factor, "row", axis=0, tiled=True)
    A, I, J = tensor.shape
    inner = jnp.dot(tensor.reshape(A * I, J), columns, preferred_element_type=f32).reshape(A, I, -1)
    row_total = jnp.sum(inner * aux_factor.astype(f32)[:, None, :], axis=0)
    aux_total = jnp.sum(inner * row_panel[None], axis=1)
    row_result = lax.psum_scatter(row_total, "col", scatter_dimension=0, tiled=True)
    scattered = lax.psum_scatter(aux_total, "row", scatter_dimension=0, tiled=True)
    return row_result, lax.psum(scattered, "col")


def solution(mesh):
    R, C = mesh.shape["row"], mesh.shape["col"]

    def body(tensor, aux, rowf, colf):
        A, I, J = tensor.shape
        jb, N = colf.shape
        ib = rowf.shape[0]
        fits = (C == 2 and R % 4 == 0 and A % (8 * R) == 0 and ib % 16 == 0 and jb % 16 == 0
                and J % 256 == 0 and N % 128 == 0 and 2 * tensor.size < 36 * 2**20)
        if fits:
            return tuple(fused(R, C, tensor, aux, rowf, colf))
        return plain(tensor, aux, rowf, colf)

    return jax.shard_map(
        body,
        mesh=mesh,
        in_specs=(
            P(None, "row", "col"),
            P(None, "rank"),
            P(("row", "col"), "rank"),
            P(("col", "row"), "rank"),
        ),
        out_specs=(P(("row", "col"), "rank"), P("row", "rank")),
        check_vma=False,
    )
```

profile of v0, /device:TPU:0, one launch (start us, length us, event | category | flops | bytes accessed | tf_op | source)
XLA Modules:
  0.0 24.7 jit_solution(8897457374966734130)
XLA Ops:
  0.6 22.5 %shard_map.59.both = f32[136,128]{1,0:T(8,128)} custom-call(bf16[64,256,1024]{2,1,0:T(8,128)(2,1)} %tensor.1, bf16[64,128]{1,0:T(8,128)(2,1)} %aux.1, bf16[128,128]{1,0:T(8,128)(2,1)} %rowf.1, bf16[128,128]{1,0:T(8,128)(2,1)} %colf.1), custom_call_target="tpu_custom_call" | custom-call | tf_op jit(solution)/shard_map/pallas_call | solution.py:191
  23.1 1.5 %shard_map.60 = (f32[128,128]{1,0:T(8,128)}, f32[8,128]{1,0:T(8,128)}) custom-call(f32[136,128]{1,0:T(8,128)} %shard_map.59.both), custom_call_target="tpu_custom_call" | custom-call | tf_op jit(solution)/shard_map/pallas_call | solution.py:214
where the time goes:
time: 24.9 us; the launch traced here: 24.7 us
  Pallas kernels  24 us (96%)
  between operations  0.64 us (3%)
    pallas_call x1, Pallas kernels, fused(): pl.pallas_call(functools.partial(kernel, R, C), out_shape=jax.ShapeDtypeS...  22.5 us
    pallas_call x1, Pallas kernels, fused(): pl.pallas_call(split, out_shape=(jax.ShapeDtypeStruct((ib, N), f32), jax....  1.52 us

commit v1 on v0

v1 whole, which is shorter than its diff:
```python
import functools

import jax
import jax.numpy as jnp
from jax import lax
from jax.experimental import pallas as pl
from jax.experimental.pallas import tpu as pltpu
from jax.sharding import PartitionSpec as P

MESH = pl.DeviceIdType.MESH
f32 = jnp.float32
scope = jax.named_scope


def kernel(R, C, Y, G, tensor, aux, rowf, colf, row_out, aux_out,
           tbuf0, tbuf1, tbuf2, colbuf, rowsrc, rowbuf, auxbuf, row_panel, aux_panel, row_acc, aux_acc, row_in, aux_in,
           t_sem, l_sem, c_send, z_recv, plane_recv, r_send, r_recv, x_send, x_recv, a_send, a_recv, p_send, p_recv):
    r = lax.axis_index("row")
    c = lax.axis_index("col")
    y = lax.axis_index("rank")
    A, I, J = tensor.shape
    jb, N = colf.shape
    ib = rowf.shape[0]
    ac = A // R
    H = R // 2
    ZH = H // 2
    half = r // H
    local = lax.rem(r, H)
    zl = local // 2
    x = lax.rem(local, 2)
    home = c == y

    def at(row, col, rank):
        return {"row": row, "col": col, "rank": rank}

    def signal(where):
        pl.semaphore_signal(barrier, inc=1, device_id=where, device_id_type=MESH)

    def settle(ref, sem):
        pltpu.make_async_copy(ref, ref, sem).wait()

    def remote(src, dst, send_sem, recv_sem, where):
        return pltpu.make_async_remote_copy(
            src_ref=src, dst_ref=dst, send_sem=send_sem, recv_sem=recv_sem, device_id=where, device_id_type=MESH)

    def slot(row, rank):
        return rank * R + row

    z = r // 2
    beside = half * ZH + lax.rem(zl + 1, ZH)
    nearer = (1 - half) * ZH + half * (ZH - 1)
    farther = (1 - half) * ZH + (1 - half) * (ZH - 1)
    columns = [(beside * 2 + x, 1), (nearer * 2 + x, 2), (farther * 2 + x, 2)]
    plane = [(z * 2 + 1 - x, 1 - y), (z * 2 + 1 - x, y), (r, 1 - y)]

    barrier = pltpu.get_barrier_semaphore()
    for row, _ in columns[::-1]:
        signal(at(row, c, y))
    for row, rank in plane:
        signal(at(row, c, rank))
    signal(at(r, 1 - c, 1 - y))
    signal(at(r, 1 - c, y))

    own_col = pltpu.make_async_copy(colf, colbuf.at[slot(r, y)], l_sem.at[0])
    own_row = pltpu.make_async_copy(rowf, rowsrc, l_sem.at[1])
    own_aux = pltpu.make_async_copy(aux, auxbuf.at[y], l_sem.at[2])
    own_col.start()
    own_row.start()
    own_aux.start()

    def order(s):
        t = s - H
        far = (1 - half) * (R - 1 - s) + half * s
        near = half * H + lax.rem(zl + 1 + lax.div(t, 2), ZH) * 2 + lax.rem(x + 1 + t, 2)
        return jnp.where(s < H, far, near)

    starts = [z * 2, beside * 2, (1 - half) * H]
    buffers = [tbuf0, tbuf1, tbuf2]
    def fetch(p):
        width = buffers[p].shape[-1]
        for s in range(R):
            pltpu.make_async_copy(
                tensor.at[pl.ds(order(s) * ac, ac), pl.ds(pl.multiple_of(y * ib, ib), ib),
                          pl.ds(pl.multiple_of(starts[p] * jb, jb), width)],
                buffers[p].at[s], t_sem.at[p]).start()

    for p in range(3):
        fetch(p)

    def to_plane(row, kind):
        ref = colbuf.at[slot(row, y)]
        for there, rank in plane:
            remote(ref, ref, c_send, plane_recv.at[kind], at(there, c, rank)).start()

    def row_copy(e):
        return remote(rowsrc, rowbuf.at[y], r_send.at[e], r_recv.at[y], at(r, e, c))

    swap = remote(auxbuf.at[y], auxbuf.at[y], x_send, x_recv, at(r, c, 1 - y))

    def small():
        swap.start()
        row_copy(1 - c).start()

        @pl.when(jnp.logical_not(home))
        def _():
            row_copy(c).start()

    with scope("ownwait"):
        own_col.wait()
        own_row.wait()
        own_aux.wait()
    with scope("barwait"):
        pl.semaphore_wait(barrier, 8)
    def along():
        ref = colbuf.at[slot(r, y)]
        for row, _ in columns:
            remote(ref, ref, c_send, z_recv.at[z], at(row, c, y)).start()

    small()
    along()
    to_plane(r, 0)

    @pl.when(home)
    def _():
        rowbuf[y] = rowsrc[...]

    row_acc[...] = jnp.zeros_like(row_acc)
    aux_acc[...] = jnp.zeros_like(aux_acc)
    def relay(which):
        for row, kind in which:
            with scope("zwait%d" % kind):
                settle(colbuf.at[slot(row, y)], z_recv.at[row // 2])
            to_plane(row, kind)

    relay(columns[:1])
    with scope("rowwait"):
        settle(auxbuf.at[1 - y], x_recv)
        settle(rowbuf.at[1 - y], r_recv.at[1 - y])

        @pl.when(jnp.logical_not(home))
        def _():
            settle(rowbuf.at[y], r_recv.at[y])

    for s in range(Y):
        row_panel[:, s * N:(s + 1) * N] = rowbuf[s].astype(f32)
        aux_panel[:, :, s * N:(s + 1) * N] = auxbuf[s].astype(f32).reshape(R, ac, N)

    def block(p, s):
        buffer = buffers[p]
        width = buffer.shape[-1]
        weights = jnp.concatenate(
            [colbuf[pl.ds(slot(starts[p], q), width // jb)].reshape(width, N) for q in range(Y)], axis=1)
        inner = jnp.dot(buffer[pl.ds(s * G, G)].reshape(G * ac * ib, width), weights, preferred_element_type=f32)
        inner = inner.reshape(G * ac, ib, Y * N)
        scale = jnp.concatenate([aux_panel[order(s * G + g)] for g in range(G)], axis=0)
        rows = jnp.sum(inner * scale[:, None, :], axis=0)
        auxs = jnp.sum(inner * row_panel[...][None], axis=1)
        for q in range(Y):
            row_acc[q] += rows[:, q * N:(q + 1) * N]
            aux_acc[pl.ds(s * G, G), q] += auxs[:, q * N:(q + 1) * N].reshape(G, ac, N)

    def place(row, col, rank):
        return (row * C + col) * Y + rank

    def aux_copy(s, e, q):
        return remote(aux_acc.at[s, q], aux_in.at[place(r, c, y)], a_send, a_recv, at(order(s), e, q))

    def step(p, s):
        block(p, s)
        if p == 2:
            for g in range(G):
                for e in range(C):
                    for q in range(Y):
                        aux_copy(s * G + g, e, q).start()
        return 0

    for p in range(3):
        with scope("wait%d" % p):
            settle(colbuf.at[pl.ds(0, 3 * max(p, 1))], plane_recv.at[p])
        with scope("load%d" % p):
            settle(buffers[p], t_sem.at[p])
        with scope("pass%d" % p):
            if p == 0:
                lax.fori_loop(0, 1, lambda s, _: step(p, s), 0)
                relay(columns[1:])
                lax.fori_loop(1, R // G, lambda s, _: step(p, s), 0)
            else:
                lax.fori_loop(0, R // G - (p == 2), lambda s, _: step(p, s), 0)
    with scope("last"):
        block(2, R // G - 1)

    def part_copy(q):
        return remote(row_acc.at[q], row_in.at[c], p_send.at[q], p_recv.at[c], at(r, y, q))

    part_copy(1 - y).start()

    @pl.when(home)
    def _():
        row_in[c] = row_acc[y]

    @pl.when(jnp.logical_not(home))
    def _():
        part_copy(y).start()

    for s in range(R - G, R - 1):
        for e in range(C):
            for q in range(Y):
                aux_copy(s, e, q).start()
    for e, q in [(1 - c, 1 - y), (c, 1 - y), (1 - c, y)]:
        aux_copy(R - 1, e, q).start()
    pltpu.make_async_copy(aux_acc.at[R - 1, y], aux_in.at[place(r, c, y)], a_recv).start()
    with scope("partwait"):
        settle(row_in.at[1 - c], p_recv.at[1 - c])

        @pl.when(jnp.logical_not(home))
        def _():
            settle(row_in.at[c], p_recv.at[c])

    row_out[...] = row_in[0] + row_in[1]
    with scope("auxwait"):
        settle(aux_in, a_recv)
    aux_out[...] = jnp.sum(aux_in[...], axis=0)

    with scope("sendwait"):
        settle(colbuf.at[pl.ds(0, Y * R - 1)], c_send)
        settle(auxbuf.at[y], x_send)
        settle(rowsrc, r_send.at[1 - c])
        settle(row_in.at[0], p_send.at[1 - y])

        @pl.when(jnp.logical_not(home))
        def _():
            settle(rowsrc, r_send.at[c])
            settle(row_in.at[0], p_send.at[y])

        settle(aux_in.at[pl.ds(0, R * C * Y - 1)], a_send)


def emit(rows, auxs, row_out, aux_out, sem):
    copies = [pltpu.make_async_copy(rows, row_out, sem.at[0]), pltpu.make_async_copy(auxs, aux_out, sem.at[1])]
    for copy in copies:
        copy.start()
    for copy in copies:
        copy.wait()


GROUP = 2


def fused(R, C, Y, tensor, aux, rowf, colf):
    A, I, J = tensor.shape
    jb, N = colf.shape
    ib = rowf.shape[0]
    ac = A // R
    bf16 = tensor.dtype
    anywhere = pl.BlockSpec(memory_space=pltpu.HBM)
    vmem = pl.BlockSpec(memory_space=pltpu.VMEM)
    dma = pltpu.SemaphoreType.DMA
    outs = pl.pallas_call(
        functools.partial(kernel, R, C, Y, GROUP),
        out_shape=(pltpu.VMEM((ib, N), f32), pltpu.VMEM((ac, N), f32)),
        in_specs=[anywhere] * 4,
        out_specs=(vmem, vmem),
        scratch_shapes=[
            pltpu.VMEM((R, ac, ib, 2 * jb), bf16),
            pltpu.VMEM((R, ac, ib, 2 * jb), bf16),
            pltpu.VMEM((R, ac, ib, J // 2), bf16),
            pltpu.VMEM((Y * R, jb, N), bf16),
            pltpu.VMEM((ib, N), bf16),
            pltpu.VMEM((Y, ib, N), bf16),
            pltpu.VMEM((Y, A, N), bf16),
            pltpu.VMEM((ib, Y * N), f32),
            pltpu.VMEM((R, ac, Y * N), f32),
            pltpu.VMEM((Y, ib, N), f32),
            pltpu.VMEM((R, Y, ac, N), f32),
            pltpu.VMEM((C, ib, N), f32),
            pltpu.VMEM((R * C * Y, ac, N), f32),
            dma((3,)), dma((3,)), dma, dma((R // 2,)), dma((3,)), dma((C,)), dma((Y,)), dma, dma, dma, dma, dma((Y,)), dma((C,)),
        ],
        compiler_params=pltpu.CompilerParams(
            collective_id=0, has_side_effects=True, vmem_limit_bytes=56 * 2**20),
    )(tensor, aux, rowf, colf)
    outs = [pltpu.with_memory_space_constraint(o, pltpu.VMEM) for o in outs]
    return pl.pallas_call(
        emit,
        out_shape=(jax.ShapeDtypeStruct((ib, N), f32), jax.ShapeDtypeStruct((ac, N), f32)),
        in_specs=[vmem] * 2,
        out_specs=(anywhere, anywhere),
        scratch_shapes=[dma((2,))],
    )(*outs)


def plain(tensor, aux_factor, row_factor, col_factor):
    row_panel = lax.all_gather(row_factor, "col", axis=0, tiled=True).astype(f32)
    columns = lax.all_gather(col_factor, "row", axis=0, tiled=True)
    A, I, J = tensor.shape
    inner = jnp.dot(tensor.reshape(A * I, J), columns, preferred_element_type=f32).reshape(A, I, -1)
    row_total = jnp.sum(inner * aux_factor.astype(f32)[:, None, :], axis=0)
    aux_total = jnp.sum(inner * row_panel[None], axis=1)
    row_result = lax.psum_scatter(row_total, "col", scatter_dimension=0, tiled=True)
    scattered = lax.psum_scatter(aux_total, "row", scatter_dimension=0, tiled=True)
    return row_result, lax.psum(scattered, "col")


def solution(mesh):
    R, C, Y = mesh.shape["row"], mesh.shape["col"], mesh.shape["rank"]

    def body(tensor, aux, rowf, colf):
        A, I, J = tensor.shape
        jb, N = colf.shape
        ib = rowf.shape[0]
        fits = (C == 2 and Y == 2 and R // 4 == 2 and R % 4 == 0 and A % (8 * R) == 0 and ib % 16 == 0 and jb % 16 == 0
                and J % 256 == 0 and N % 128 == 0 and tensor.size < 24 * 2**20)
        if fits:
            return tuple(fused(R, C, Y, tensor, aux, rowf, colf))
        return plain(tensor, aux, rowf, colf)

    return jax.shard_map(
        body,
        mesh=mesh,
        in_specs=(
            P(None, "row", "col"),
            P(None, "rank"),
            P(("row", "col"), "rank"),
            P(("col", "row"), "rank"),
        ),
        out_specs=(P(("row", "col"), "rank"), P("row", "rank")),
        check_vma=False,
    )
```

time: 24.9 us -> 23.8 us (0.956)
  Pallas kernels: 24 us -> 23 us
    pallas_call x2, Pallas kernels: 24 us -> 23 us  [the longest x1 22.3 us: fused(): pl.pallas_call(functools.partial(kernel, R, C, Y, GROUP), out_shape=(pltp...]
where the time goes in v1:
time: 23.8 us; the launch traced here: 23.6 us
  Pallas kernels  23 us (97%)
  between operations  0.64 us (3%)
    pallas_call x1, Pallas kernels, fused(): pl.pallas_call(functools.partial(kernel, R, C, Y, GROUP), out_shape=(pltp...  22.3 us
    pallas_call x1, Pallas kernels, fused(): pl.pallas_call(emit, out_shape=(jax.ShapeDtypeStruct((ib, N), f32), jax.S...  0.65 us

profile of v1, /device:TPU:0, one launch (start us, length us, event | category | flops | bytes accessed | tf_op | source)
XLA Modules:
  0.0 23.6 jit_solution(16606424629369517873)
XLA Ops:
  0.6 22.3 %shard_map.59 = (f32[128,128]{1,0:T(8,128)S(1)}, f32[8,128]{1,0:T(8,128)S(1)}) custom-call(bf16[64,256,1024]{2,1,0:T(8,128)(2,1)} %tensor.1, bf16[64,128]{1,0:T(8,128)(2,1)} %aux.1, bf16[128,128]{1,0:T(8,128)(2,1)} %rowf.1, bf16[128,128]{1,0:T(8,128)(2,1)} %colf.1), custom_call_target="tpu_custom_call" | custom-call | tf_op jit(solution)/shard_map/pallas_call | solution.py:258
  23.0 0.7 %shard_map.60 = (f32[128,128]{1,0:T(8,128)}, f32[8,128]{1,0:T(8,128)}) custom-call(f32[128,128]{1,0:T(8,128)S(1)} %get-tuple-element.4.rows, f32[8,128]{1,0:T(8,128)S(1)} %get-tuple-element.5.auxs), custom_call_target="tpu_custom_call" | custom-call | tf_op jit(solution)/shard_map/pallas_call | solution.py:283

commit v2 on v1

v2 whole, which is shorter than its diff:
```python
import functools

import jax
import jax.numpy as jnp
from jax import lax
from jax.experimental import pallas as pl
from jax.experimental.pallas import tpu as pltpu
from jax.sharding import PartitionSpec as P

MESH = pl.DeviceIdType.MESH
f32 = jnp.float32
scope = jax.named_scope


def kernel(R, C, Y, tensor, aux, rowf, colf, row_out, aux_out,
           tbuf0, tbuf1, colbuf, rowsrc, rowbuf, auxbuf, row_panel, aux_panel, row_acc, aux_acc, row_in, aux_in,
           t_sem, l_sem, c_send, z_recv, near_recv, far_recv, r_send, r_recv, x_send, x_recv, a_send, a_recv, p_send, p_recv):
    r = lax.axis_index("row")
    c = lax.axis_index("col")
    y = lax.axis_index("rank")
    A, I, J = tensor.shape
    jb, N = colf.shape
    ib = rowf.shape[0]
    ac = A // R
    H = R // 2
    ZH = H // 2
    half = r // H
    local = lax.rem(r, H)
    zl = local // 2
    x = lax.rem(local, 2)
    home = c == y
    away = c != y

    def at(row, col, rank):
        return {"row": row, "col": col, "rank": rank}

    def signal(where):
        pl.semaphore_signal(barrier, inc=1, device_id=where, device_id_type=MESH)

    def settle(ref, sem):
        pltpu.make_async_copy(ref, ref, sem).wait()

    def remote(src, dst, send_sem, recv_sem, where):
        return pltpu.make_async_remote_copy(
            src_ref=src, dst_ref=dst, send_sem=send_sem, recv_sem=recv_sem, device_id=where, device_id_type=MESH)

    def slot(row, rank):
        return rank * R + row

    z = r // 2
    beside = half * ZH + lax.rem(zl + 1, ZH)
    nearer = (1 - half) * ZH + half * (ZH - 1)
    farther = (1 - half) * ZH + (1 - half) * (ZH - 1)
    columns = [nearer * 2 + x, farther * 2 + x]
    plane = [(z * 2 + 1 - x, 1 - y), (z * 2 + 1 - x, y), (r, 1 - y)]
    next_plane = [(beside * 2 + 1 - x, 1 - y), (beside * 2 + 1 - x, y), (beside * 2 + x, 1 - y), (beside * 2 + x, y)]

    barrier = pltpu.get_barrier_semaphore()
    for row in columns[::-1]:
        signal(at(row, c, y))
    for row, rank in next_plane + plane:
        signal(at(row, c, rank))
    signal(at(r, 1 - c, 1 - y))
    signal(at(r, 1 - c, y))

    own_col = pltpu.make_async_copy(colf, colbuf.at[slot(r, y)], l_sem.at[0])
    own_row = pltpu.make_async_copy(rowf, rowsrc, l_sem.at[1])
    own_aux = pltpu.make_async_copy(aux, auxbuf.at[y], l_sem.at[2])
    own_col.start()
    own_row.start()
    own_aux.start()

    def order(s):
        t = s - H
        far = (1 - half) * (R - 1 - s) + half * s
        near = half * H + lax.rem(zl + 1 + lax.div(t, 2), ZH) * 2 + lax.rem(x + 1 + t, 2)
        return jnp.where(s < H, far, near)

    starts = [half * H, (1 - half) * H]
    buffers = [tbuf0, tbuf1]
    def fetch(p):
        width = buffers[p].shape[-1]
        for s in range(R):
            pltpu.make_async_copy(
                tensor.at[pl.ds(order(s) * ac, ac), pl.ds(pl.multiple_of(y * ib, ib), ib),
                          pl.ds(pl.multiple_of(starts[p] * jb, jb), width)],
                buffers[p].at[s], t_sem.at[p]).start()

    for p in range(2):
        fetch(p)

    def block_copy(source, recv_sem, where):
        ref = colbuf.at[slot(source, y)]
        return remote(ref, ref, c_send, recv_sem, where)

    def row_copy(src, q, col, rank):
        return remote(src, rowbuf.at[q], r_send, r_recv.at[q], at(r, col, rank))

    def aux_swap(q, col, rank):
        return remote(auxbuf.at[q], auxbuf.at[q], x_send, x_recv, at(r, col, rank))

    def small():
        @pl.when(home)
        def _():
            aux_swap(y, c, 1 - y).start()
            row_copy(rowsrc, y, 1 - c, y).start()

        @pl.when(away)
        def _():
            row_copy(rowsrc, y, c, 1 - y).start()

    def pass_on():
        @pl.when(home)
        def _():
            rowbuf[y] = rowsrc[...]
            settle(rowbuf.at[1 - y], r_recv.at[1 - y])
            row_copy(rowbuf.at[1 - y], 1 - y, 1 - c, y).start()

        @pl.when(away)
        def _():
            settle(auxbuf.at[1 - y], x_recv)
            aux_swap(1 - y, 1 - c, y).start()

    def small_arrival():
        @pl.when(home)
        def _():
            settle(auxbuf.at[1 - y], x_recv)

        @pl.when(away)
        def _():
            for q in range(Y):
                settle(rowbuf.at[q], r_recv.at[q])

    with scope("ownwait"):
        own_col.wait()
        own_row.wait()
        own_aux.wait()
    with scope("barwait"):
        pl.semaphore_wait(barrier, 11)
    small()
    for row in columns:
        block_copy(r, z_recv.at[z], at(row, c, y)).start()
    for row, rank in next_plane + plane:
        block_copy(r, near_recv, at(row, c, rank)).start()

    row_acc[...] = jnp.zeros_like(row_acc)
    aux_acc[...] = jnp.zeros_like(aux_acc)
    def relay():
        for row in columns:
            with scope("zwait"):
                settle(colbuf.at[slot(row, y)], z_recv.at[row // 2])
            for there, rank in plane:
                block_copy(row, far_recv, at(there, c, rank)).start()

    pass_on()
    relay()
    with scope("rowwait"):
        small_arrival()

    for s in range(Y):
        row_panel[:, s * N:(s + 1) * N] = rowbuf[s].astype(f32)
        aux_panel[:, :, s * N:(s + 1) * N] = auxbuf[s].astype(f32).reshape(R, ac, N)

    def block(p, s, G, i, span):
        buffer = buffers[p]
        width = buffer.shape[-1]
        i = pl.multiple_of(i, span)
        weights = jnp.concatenate(
            [colbuf[pl.ds(slot(starts[p], q), width // jb)].reshape(width, N) for q in range(Y)], axis=1)
        tiles = buffer[pl.ds(s, G), :, pl.ds(i, span), :].reshape(G * ac * span, width)
        inner = jnp.dot(tiles, weights, preferred_element_type=f32).reshape(G * ac, span, Y * N)
        scale = jnp.concatenate([aux_panel[order(s + g)] for g in range(G)], axis=0)
        rows = jnp.sum(inner * scale[:, None, :], axis=0)
        auxs = jnp.sum(inner * row_panel[pl.ds(i, span), :][None], axis=1)
        for q in range(Y):
            row_acc[q, pl.ds(i, span), :] += rows[:, q * N:(q + 1) * N]
            aux_acc[pl.ds(s, G), q] += auxs[:, q * N:(q + 1) * N].reshape(G, ac, N)

    def place(row, col, rank):
        return (row * C + col) * Y + rank

    def aux_copy(s, e, q):
        return remote(aux_acc.at[s, q], aux_in.at[place(r, c, y)], a_send, a_recv, at(order(s), e, q))

    others = [(1 - c, 1 - y), (c, 1 - y), (1 - c, y)]

    def spread(s, G):
        for g in range(G):
            for e, q in others + [(c, y)]:
                aux_copy(s + g, e, q).start()

    def part_copy(q, i, span):
        part = pl.ds(i, span)
        return remote(row_acc.at[q, part], row_in.at[c, part], p_send.at[q], p_recv.at[c], at(r, y, q))

    def parts(i, span):
        i = pl.multiple_of(i, span)
        part_copy(1 - y, i, span).start()

        @pl.when(away)
        def _():
            part_copy(y, i, span).start()

    with scope("wait0"):
        settle(colbuf.at[pl.ds(0, 7)], near_recv)
    with scope("load0"):
        settle(tbuf0, t_sem.at[0])
    def first(s, _):
        block(0, s * G0, G0, 0, ib)
        return 0

    def second(s, _):
        block(1, s * G2, G2, 0, ib)

        @pl.when(s < R // G2 - 1)
        def _():
            spread(s * G2, G2)

        return 0

    with scope("pass0"):
        lax.fori_loop(0, R // G0, first, 0)
    with scope("wait1"):
        settle(colbuf.at[pl.ds(0, 6)], far_recv)
        settle(tbuf1, t_sem.at[1])
    with scope("pass1"):
        lax.fori_loop(0, R // G2, second, 0)
    parts(0, ib)

    spread(R - G2, G2 - 1)
    for e, q in others:
        aux_copy(R - 1, e, q).start()

    @pl.when(home)
    def _():
        row_in[c] = row_acc[y]

    pltpu.make_async_copy(aux_acc.at[R - 1, y], aux_in.at[place(r, c, y)], a_recv).start()
    with scope("partwait"):
        settle(row_in.at[1 - c], p_recv.at[1 - c])

        @pl.when(away)
        def _():
            settle(row_in.at[c], p_recv.at[c])

    row_out[...] = row_in[0] + row_in[1]
    with scope("auxwait"):
        settle(aux_in, a_recv)
    aux_out[...] = jnp.sum(aux_in[...], axis=0)

    with scope("sendwait"):
        settle(colbuf.at[pl.ds(0, Y * R - 1)], c_send)
        settle(auxbuf.at[y], x_send)
        settle(row_in.at[0], p_send.at[1 - y])

        @pl.when(away)
        def _():
            settle(rowsrc, r_send)
            settle(row_in.at[0], p_send.at[y])

        @pl.when(home)
        def _():
            settle(rowbuf, r_send)

        settle(aux_in.at[pl.ds(0, R * C * Y - 1)], a_send)


def emit(rows, auxs, row_out, aux_out, sem):
    copies = [pltpu.make_async_copy(rows, row_out, sem.at[0]), pltpu.make_async_copy(auxs, aux_out, sem.at[1])]
    for copy in copies:
        copy.start()
    for copy in copies:
        copy.wait()


G0 = 4
G2 = 4


def fused(R, C, Y, tensor, aux, rowf, colf):
    A, I, J = tensor.shape
    jb, N = colf.shape
    ib = rowf.shape[0]
    ac = A // R
    bf16 = tensor.dtype
    anywhere = pl.BlockSpec(memory_space=pltpu.HBM)
    vmem = pl.BlockSpec(memory_space=pltpu.VMEM)
    dma = pltpu.SemaphoreType.DMA
    outs = pl.pallas_call(
        functools.partial(kernel, R, C, Y),
        out_shape=(pltpu.VMEM((ib, N), f32), pltpu.VMEM((ac, N), f32)),
        in_specs=[anywhere] * 4,
        out_specs=(vmem, vmem),
        scratch_shapes=[
            pltpu.VMEM((R, ac, ib, J // 2), bf16),
            pltpu.VMEM((R, ac, ib, J // 2), bf16),
            pltpu.VMEM((Y * R, jb, N), bf16),
            pltpu.VMEM((ib, N), bf16),
            pltpu.VMEM((Y, ib, N), bf16),
            pltpu.VMEM((Y, A, N), bf16),
            pltpu.VMEM((ib, Y * N), f32),
            pltpu.VMEM((R, ac, Y * N), f32),
            pltpu.VMEM((Y, ib, N), f32),
            pltpu.VMEM((R, Y, ac, N), f32),
            pltpu.VMEM((C, ib, N), f32),
            pltpu.VMEM((R * C * Y, ac, N), f32),
            dma((2,)), dma((3,)), dma, dma((R // 2,)), dma, dma, dma, dma((Y,)), dma, dma, dma, dma, dma((Y,)), dma((C,)),
        ],
        compiler_params=pltpu.CompilerParams(
            collective_id=0, has_side_effects=True, vmem_limit_bytes=56 * 2**20),
    )(tensor, aux, rowf, colf)
    outs = [pltpu.with_memory_space_constraint(o, pltpu.VMEM) for o in outs]
    return pl.pallas_call(
        emit,
        out_shape=(jax.ShapeDtypeStruct((ib, N), f32), jax.ShapeDtypeStruct((ac, N), f32)),
        in_specs=[vmem] * 2,
        out_specs=(anywhere, anywhere),
        scratch_shapes=[dma((2,))],
    )(*outs)


def plain(tensor, aux_factor, row_factor, col_factor):
    row_panel = lax.all_gather(row_factor, "col", axis=0, tiled=True).astype(f32)
    columns = lax.all_gather(col_factor, "row", axis=0, tiled=True)
    A, I, J = tensor.shape
    inner = jnp.dot(tensor.reshape(A * I, J), columns, preferred_element_type=f32).reshape(A, I, -1)
    row_total = jnp.sum(inner * aux_factor.astype(f32)[:, None, :], axis=0)
    aux_total = jnp.sum(inner * row_panel[None], axis=1)
    row_result = lax.psum_scatter(row_total, "col", scatter_dimension=0, tiled=True)
    scattered = lax.psum_scatter(aux_total, "row", scatter_dimension=0, tiled=True)
    return row_result, lax.psum(scattered, "col")


def solution(mesh):
    R, C, Y = mesh.shape["row"], mesh.shape["col"], mesh.shape["rank"]

    def body(tensor, aux, rowf, colf):
        A, I, J = tensor.shape
        jb, N = colf.shape
        ib = rowf.shape[0]
        fits = (C == 2 and Y == 2 and R // 4 == 2 and R % 4 == 0 and A % (8 * R) == 0 and ib % 16 == 0 and jb % 16 == 0
                and J % 256 == 0 and N % 128 == 0 and tensor.size < 24 * 2**20)
        if fits:
            return tuple(fused(R, C, Y, tensor, aux, rowf, colf))
        return plain(tensor, aux, rowf, colf)

    return jax.shard_map(
        body,
        mesh=mesh,
        in_specs=(
            P(None, "row", "col"),
            P(None, "rank"),
            P(("row", "col"), "rank"),
            P(("col", "row"), "rank"),
        ),
        out_specs=(P(("row", "col"), "rank"), P("row", "rank")),
        check_vma=False,
    )
```

time: 23.8 us -> 22.8 us (0.958)
  Pallas kernels: 23 us -> 22 us
    pallas_call x1, Pallas kernels: 22.3 us -> 21.3 us  [fused(): pl.pallas_call(functools.partial(kernel, R, C, Y), out_shape=(pltpu.VMEM(...]
where the time goes in v2:
time: 22.8 us; the launch traced here: 22.6 us
  Pallas kernels  22 us (96%)
  between operations  0.64 us (3%)
    pallas_call x1, Pallas kernels, fused(): pl.pallas_call(functools.partial(kernel, R, C, Y), out_shape=(pltpu.VMEM(...  21.3 us
    pallas_call x1, Pallas kernels, fused(): pl.pallas_call(emit, out_shape=(jax.ShapeDtypeStruct((ib, N), f32), jax.S...  0.65 us

profile of v2, /device:TPU:0, one launch (start us, length us, event | category | flops | bytes accessed | tf_op | source)
XLA Modules:
  0.0 22.6 jit_solution(14679267769600631032)
XLA Ops:
  0.6 21.3 %shard_map.59 = (f32[128,128]{1,0:T(8,128)S(1)}, f32[8,128]{1,0:T(8,128)S(1)}) custom-call(bf16[64,256,1024]{2,1,0:T(8,128)(2,1)} %tensor.1, bf16[64,128]{1,0:T(8,128)(2,1)} %aux.1, bf16[128,128]{1,0:T(8,128)(2,1)} %rowf.1, bf16[128,128]{1,0:T(8,128)(2,1)} %colf.1), custom_call_target="tpu_custom_call" | custom-call | tf_op jit(solution)/shard_map/pallas_call | solution.py:289
  22.0 0.7 %shard_map.60 = (f32[128,128]{1,0:T(8,128)}, f32[8,128]{1,0:T(8,128)}) custom-call(f32[128,128]{1,0:T(8,128)S(1)} %get-tuple-element.4.rows, f32[8,128]{1,0:T(8,128)S(1)} %get-tuple-element.5.auxs), custom_call_target="tpu_custom_call" | custom-call | tf_op jit(solution)/shard_map/pallas_call | solution.py:313

commit v3 on v2

--- a/solution.py
+++ b/solution.py
@@ -13,7 +13,7 @@
 
 
 def kernel(R, C, Y, tensor, aux, rowf, colf, row_out, aux_out,
-           tbuf0, tbuf1, colbuf, rowsrc, rowbuf, auxbuf, row_panel, aux_panel, row_acc, aux_acc, row_in, aux_in,
+           tbuf0, tbuf1, tbuf2, colbuf, rowsrc, rowbuf, auxbuf, row_panel, aux_panel, row_acc, aux_acc, row_in, aux_in,
            t_sem, l_sem, c_send, z_recv, near_recv, far_recv, r_send, r_recv, x_send, x_recv, a_send, a_recv, p_send, p_recv):
     r = lax.axis_index("row")
     c = lax.axis_index("col")
@@ -51,14 +51,13 @@
     beside = half * ZH + lax.rem(zl + 1, ZH)
     nearer = (1 - half) * ZH + half * (ZH - 1)
     farther = (1 - half) * ZH + (1 - half) * (ZH - 1)
-    columns = [nearer * 2 + x, farther * 2 + x]
+    columns = [beside * 2 + x, nearer * 2 + x, farther * 2 + x]
     plane = [(z * 2 + 1 - x, 1 - y), (z * 2 + 1 - x, y), (r, 1 - y)]
-    next_plane = [(beside * 2 + 1 - x, 1 - y), (beside * 2 + 1 - x, y), (beside * 2 + x, 1 - y), (beside * 2 + x, y)]
 
     barrier = pltpu.get_barrier_semaphore()
     for row in columns[::-1]:
         signal(at(row, c, y))
-    for row, rank in next_plane + plane:
+    for row, rank in plane:
         signal(at(row, c, rank))
     signal(at(r, 1 - c, 1 - y))
     signal(at(r, 1 - c, y))
@@ -76,8 +75,8 @@
         near = half * H + lax.rem(zl + 1 + lax.div(t, 2), ZH) * 2 + lax.rem(x + 1 + t, 2)
         return jnp.where(s < H, far, near)
 
-    starts = [half * H, (1 - half) * H]
-    buffers = [tbuf0, tbuf1]
+    starts = [z * 2, beside * 2, (1 - half) * H]
+    buffers = [tbuf0, tbuf1, tbuf2]
     def fetch(p):
         width = buffers[p].shape[-1]
         for s in range(R):
@@ -86,7 +85,7 @@
                           pl.ds(pl.multiple_of(starts[p] * jb, jb), width)],
                 buffers[p].at[s], t_sem.at[p]).start()
 
-    for p in range(2):
+    for p in range(3):
         fetch(p)
 
     def block_copy(source, recv_sem, where):
@@ -136,24 +135,28 @@
         own_row.wait()
         own_aux.wait()
     with scope("barwait"):
-        pl.semaphore_wait(barrier, 11)
+        pl.semaphore_wait(barrier, 8)
     small()
-    for row in columns:
-        block_copy(r, z_recv.at[z], at(row, c, y)).start()
-    for row, rank in next_plane + plane:
-        block_copy(r, near_recv, at(row, c, rank)).start()
+    def far_sends():
+        for row in columns:
+            block_copy(r, z_recv.at[z], at(row, c, y)).start()
+
+    far_sends()
+    for row, rank in plane:
+        block_copy(r, near_recv.at[0], at(row, c, rank)).start()
 
     row_acc[...] = jnp.zeros_like(row_acc)
     aux_acc[...] = jnp.zeros_like(aux_acc)
-    def relay():
-        for row in columns:
+    def relay(rows):
+        for row in rows:
             with scope("zwait"):
                 settle(colbuf.at[slot(row, y)], z_recv.at[row // 2])
             for there, rank in plane:
-                block_copy(row, far_recv, at(there, c, rank)).start()
-
+                block_copy(row, near_recv.at[1] if row is columns[0] else far_recv, at(there, c, rank)).start()
+
+    relay(columns[:1])
     pass_on()
-    relay()
+    relay(columns[1:])
     with scope("rowwait"):
         small_arrival()
 
@@ -170,7 +173,9 @@
         tiles = buffer[pl.ds(s, G), :, pl.ds(i, span), :].reshape(G * ac * span, width)
         inner = jnp.dot(tiles, weights, preferred_element_type=f32).reshape(G * ac, span, Y * N)
         scale = jnp.concatenate([aux_panel[order(s + g)] for g in range(G)], axis=0)
-        rows = jnp.sum(inner * scale[:, None, :], axis=0)
+        scaled = inner * scale[:, None, :]
+        cut = G * ac // CHAINS
+        rows = sum(jnp.sum(scaled[n * cut:(n + 1) * cut], axis=0) for n in range(CHAINS))
         auxs = jnp.sum(inner * row_panel[pl.ds(i, span), :][None], axis=1)
         for q in range(Y):
             row_acc[q, pl.ds(i, span), :] += rows[:, q * N:(q + 1) * N]
@@ -201,16 +206,12 @@
         def _():
             part_copy(y, i, span).start()
 
-    with scope("wait0"):
-        settle(colbuf.at[pl.ds(0, 7)], near_recv)
-    with scope("load0"):
-        settle(tbuf0, t_sem.at[0])
-    def first(s, _):
-        block(0, s * G0, G0, 0, ib)
+    def near(p, s):
+        block(p, lax.div(s, SPANS) * G0, G0, lax.rem(s, SPANS) * (ib // SPANS), ib // SPANS)
         return 0
 
     def second(s, _):
-        block(1, s * G2, G2, 0, ib)
+        block(2, s * G2, G2, 0, ib)
 
         @pl.when(s < R // G2 - 1)
         def _():
@@ -218,12 +219,17 @@
 
         return 0
 
-    with scope("pass0"):
-        lax.fori_loop(0, R // G0, first, 0)
-    with scope("wait1"):
+    for p in range(2):
+        with scope("wait%d" % p):
+            settle(colbuf.at[pl.ds(0, 3)], near_recv.at[p])
+            settle(buffers[p], t_sem.at[p])
+        trips = R // G0 * SPANS
+        with scope("pass%d" % p):
+            lax.fori_loop(0, trips, lambda s, _: near(p, s), 0)
+    with scope("wait2"):
         settle(colbuf.at[pl.ds(0, 6)], far_recv)
-        settle(tbuf1, t_sem.at[1])
-    with scope("pass1"):
+        settle(buffers[2], t_sem.at[2])
+    with scope("pass2"):
         lax.fori_loop(0, R // G2, second, 0)
     parts(0, ib)
 
@@ -273,8 +279,10 @@
         copy.wait()
 
 
-G0 = 4
+G0 = 8
 G2 = 4
+SPANS = 2
+CHAINS = 2
 
 
 def fused(R, C, Y, tensor, aux, rowf, colf):
@@ -292,7 +300,8 @@
         in_specs=[anywhere] * 4,
         out_specs=(vmem, vmem),
         scratch_shapes=[
-            pltpu.VMEM((R, ac, ib, J // 2), bf16),
+            pltpu.VMEM((R, ac, ib, 2 * jb), bf16),
+            pltpu.VMEM((R, ac, ib, 2 * jb), bf16),
             pltpu.VMEM((R, ac, ib, J // 2), bf16),
             pltpu.VMEM((Y * R, jb, N), bf16),
             pltpu.VMEM((ib, N), bf16),
@@ -304,7 +313,7 @@
             pltpu.VMEM((R, Y, ac, N), f32),
             pltpu.VMEM((C, ib, N), f32),
             pltpu.VMEM((R * C * Y, ac, N), f32),
-            dma((2,)), dma((3,)), dma, dma((R // 2,)), dma, dma, dma, dma((Y,)), dma, dma, dma, dma, dma((Y,)), dma((C,)),
+            dma((3,)), dma((3,)), dma, dma((R // 2,)), dma((2,)), dma, dma, dma((Y,)), dma, dma, dma, dma, dma((Y,)), dma((C,)),
         ],
         compiler_params=pltpu.CompilerParams(
             collective_id=0, has_side_effects=True, vmem_limit_bytes=56 * 2**20),

time: 22.8 us -> 22.4 us (0.982)
  Pallas kernels: 22 us -> 21.6 us
    pallas_call x1, Pallas kernels: 21.3 us -> 21 us  [fused(): pl.pallas_call(functools.partial(kernel, R, C, Y), out_shape=(pltpu.VMEM(...]
where the time goes in v3:
time: 22.4 us; the launch traced here: 22.3 us
  Pallas kernels  21.6 us (96%)
  between operations  0.64 us (3%)
    pallas_call x1, Pallas kernels, fused(): pl.pallas_call(functools.partial(kernel, R, C, Y), out_shape=(pltpu.VMEM(...  21 us
    pallas_call x1, Pallas kernels, fused(): pl.pallas_call(emit, out_shape=(jax.ShapeDtypeStruct((ib, N), f32), jax.S...  0.65 us

profile of v3, /device:TPU:0, one launch (start us, length us, event | category | flops | bytes accessed | tf_op | source)
XLA Modules:
  0.0 22.3 jit_solution(16975392978545140472)
XLA Ops:
  0.6 21.0 %shard_map.59 = (f32[128,128]{1,0:T(8,128)S(1)}, f32[8,128]{1,0:T(8,128)S(1)}) custom-call(bf16[64,256,1024]{2,1,0:T(8,128)(2,1)} %tensor.1, bf16[64,128]{1,0:T(8,128)(2,1)} %aux.1, bf16[128,128]{1,0:T(8,128)(2,1)} %rowf.1, bf16[128,128]{1,0:T(8,128)(2,1)} %colf.1), custom_call_target="tpu_custom_call" | custom-call | tf_op jit(solution)/shard_map/pallas_call | solution.py:297
  21.6 0.7 %shard_map.60 = (f32[128,128]{1,0:T(8,128)}, f32[8,128]{1,0:T(8,128)}) custom-call(f32[128,128]{1,0:T(8,128)S(1)} %get-tuple-element.4.rows, f32[8,128]{1,0:T(8,128)S(1)} %get-tuple-element.5.auxs), custom_call_target="tpu_custom_call" | custom-call | tf_op jit(solution)/shard_map/pallas_call | solution.py:322

commit v4 on v3

--- a/solution.py
+++ b/solution.py
@@ -174,8 +174,9 @@
         inner = jnp.dot(tiles, weights, preferred_element_type=f32).reshape(G * ac, span, Y * N)
         scale = jnp.concatenate([aux_panel[order(s + g)] for g in range(G)], axis=0)
         scaled = inner * scale[:, None, :]
-        cut = G * ac // CHAINS
-        rows = sum(jnp.sum(scaled[n * cut:(n + 1) * cut], axis=0) for n in range(CHAINS))
+        chains = CHAINS if p < 2 else 1
+        cut = G * ac // chains
+        rows = sum(jnp.sum(scaled[n * cut:(n + 1) * cut], axis=0) for n in range(chains))
         auxs = jnp.sum(inner * row_panel[pl.ds(i, span), :][None], axis=1)
         for q in range(Y):
             row_acc[q, pl.ds(i, span), :] += rows[:, q * N:(q + 1) * N]
@@ -231,11 +232,11 @@
         settle(buffers[2], t_sem.at[2])
     with scope("pass2"):
         lax.fori_loop(0, R // G2, second, 0)
-    parts(0, ib)
 
     spread(R - G2, G2 - 1)
     for e, q in others:
         aux_copy(R - 1, e, q).start()
+    parts(0, ib)
 
     @pl.when(home)
     def _():

time: 22.4 us -> 22.4 us (level)
  no operation moved by 1% of the time
where the time goes in v4:
time: 22.4 us; the launch traced here: 22.2 us
  Pallas kernels  21.6 us (96%)
  between operations  0.64 us (3%)
    pallas_call x1, Pallas kernels, fused(): pl.pallas_call(functools.partial(kernel, R, C, Y), out_shape=(pltpu.VMEM(...  20.9 us
    pallas_call x1, Pallas kernels, fused(): pl.pallas_call(emit, out_shape=(jax.ShapeDtypeStruct((ib, N), f32), jax.S...  0.65 us

profile of v4, /device:TPU:0, one launch (start us, length us, event | category | flops | bytes accessed | tf_op | source)
XLA Modules:
  0.0 22.2 jit_solution(3879572103991545044)
XLA Ops:
  0.6 20.9 %shard_map.59 = (f32[128,128]{1,0:T(8,128)S(1)}, f32[8,128]{1,0:T(8,128)S(1)}) custom-call(bf16[64,256,1024]{2,1,0:T(8,128)(2,1)} %tensor.1, bf16[64,128]{1,0:T(8,128)(2,1)} %aux.1, bf16[128,128]{1,0:T(8,128)(2,1)} %rowf.1, bf16[128,128]{1,0:T(8,128)(2,1)} %colf.1), custom_call_target="tpu_custom_call" | custom-call | tf_op jit(solution)/shard_map/pallas_call | solution.py:298
  21.6 0.7 %shard_map.60 = (f32[128,128]{1,0:T(8,128)}, f32[8,128]{1,0:T(8,128)}) custom-call(f32[128,128]{1,0:T(8,128)S(1)} %get-tuple-element.4.rows, f32[8,128]{1,0:T(8,128)S(1)} %get-tuple-element.5.auxs), custom_call_target="tpu_custom_call" | custom-call | tf_op jit(solution)/shard_map/pallas_call | solution.py:323
